TPU v7x, 512 devices: a whole 4x8x8 slice. The times are simulated.
512 devices in a mesh: dp: 32 (over z, y_hi), tensor: 16 (over x, y_lo, core).
Axes of the slice: x: 4, y: 8 (y_hi: 4, y_lo: 2; y = y_hi * 2 + y_lo), z: 8, core: 2. Of those that a mesh axis runs over, the one named last changes fastest.
Arguments:
- hidden: bfloat16 [16384, 7168], P('dp', 'tensor'), may hold values from -6 to 6
- w_down: bfloat16 [7168, 576], P('tensor'), may hold values from -0.0625 to 0.0625
- norm_gain: float32 [512], replicated, may hold values from 0.25 to 1.75
- w_up: bfloat16 [512, 32768], P('dp', 'tensor'), may hold values from -0.25 to 0.25
- kv_grad: bfloat16 [16384, 32768], P('dp', 'tensor'), may hold values from -6 to 6
- rope_grad: bfloat16 [16384, 64], P('dp'), may hold values from -6 to 6
Outputs:
- hidden_grad: bfloat16 [16384, 7168], P('dp', 'tensor')
- down_grad: bfloat16 [7168, 576], P('tensor')
- gain_grad: float32 [512], replicated
- up_grad: bfloat16 [512, 32768], P('dp', 'tensor')
All inputs are finite; a program needn't handle non-finite values.
Results may differ from a plain program's by a relative error of at most 0.005.
Values may be sent and summed in bfloat16 or wider, within the bound.
No kernel may reach another device: no remote copies, remote signals or barrier semaphores. Data moves between devices by JAX's collectives and lax.ppermute only.
A program may use at most 64 MiB of HBM per device.

v0:
```python
import jax
import jax.numpy as jnp
from jax import lax
from jax.sharding import Mesh
from jax.sharding import PartitionSpec as P

ALL = ("z", "yh", "x", "yl", "core")
DP = ("z", "yh")
TENSOR = ("x", "yl", "core")
GAIN_ROWS = 8
LANES = 512


def dot(a, b, dims):
    return lax.dot_general(a, b, (dims, ((), ())), preferred_element_type=jnp.float32)


def two_halves(value):
    high = value.astype(jnp.bfloat16)
    low = (value - high.astype(jnp.float32)).astype(jnp.bfloat16)
    return (high, low)


def scatter_sum(partial, axes, parts):
    pieces = partial.reshape((parts, -1) + partial.shape[1:])
    arrived = lax.all_to_all(pieces, axes, 0, 0, tiled=True)
    return jnp.sum(arrived.astype(jnp.float32), axis=0)


def spread(piece, axes, parts):
    copies = jnp.broadcast_to(piece[None], (parts,) + piece.shape)
    return lax.all_to_all(copies, axes, 0, 0, tiled=True)


def after(value, earlier):
    return lax.optimization_barrier((value, earlier))[0]


def with_gain(down, gain):
    high, low = two_halves(gain)
    lanes = jnp.stack([high, low], axis=-2)
    rows = [(0, 0)] * (lanes.ndim - 2) + [(0, down.shape[-2] - 2), (0, 0)]
    return jnp.concatenate([down.astype(jnp.bfloat16), jnp.pad(lanes, rows)], axis=-1)


def parted(both, width):
    lanes = both[..., :2, width:].astype(jnp.float32)
    return (both[..., :width], lanes[..., 0, :] + lanes[..., 1, :])


def body(sizes, hidden, w_down, norm_gain, w_up, kv_grad, rope_grad):
    n_z, n_yh, n_t = sizes
    lat = norm_gain.shape[0]
    width = w_down.shape[1]
    w_up_near = spread(w_up, "yh", n_yh).reshape(-1, w_up.shape[1])
    w_up_all = lax.all_gather(w_up_near, "z", axis=0, tiled=True)
    projected = scatter_sum(dot(hidden, w_down[:, :lat], ((1,), (0,))), TENSOR, n_t)
    inv_rms = lax.rsqrt(jnp.mean(projected * projected, axis=1, keepdims=True) + 1e-06)
    latent = (projected * inv_rms * norm_gain).astype(jnp.bfloat16)
    latent_all = spread(latent, TENSOR, n_t).reshape(-1, lat)
    up_part = dot(latent_all, kv_grad, ((0,), (0,))).astype(jnp.bfloat16)
    up_sum = lax.psum_scatter(up_part, "z", scatter_dimension=0, tiled=True)
    grad_part = dot(kv_grad, after(w_up_all, up_part), ((1,), (1,)))
    latent_grad = scatter_sum(grad_part.astype(jnp.bfloat16), TENSOR, n_t)
    gain_share = jnp.sum(latent_grad * projected * inv_rms, axis=0)
    scaled = norm_gain * latent_grad
    proj_grad = (
        inv_rms * scaled
        - projected
        * inv_rms
        * inv_rms
        * inv_rms
        * jnp.sum(scaled * projected, axis=1, keepdims=True)
        / lat
    ).astype(jnp.bfloat16)
    high, low = two_halves(gain_share)
    fill = jnp.zeros((GAIN_ROWS - 2, lat), jnp.bfloat16)
    joined = spread(jnp.concatenate([proj_grad, high[None], low[None], fill], axis=0), TENSOR, n_t)
    rows = proj_grad.shape[0]
    joint_grad = jnp.concatenate([joined[:, :rows].reshape(-1, lat), rope_grad], axis=1)
    gain_group = jnp.sum(joined[:, rows : rows + 2].astype(jnp.float32), axis=(0, 1))
    hidden_grad = dot(joint_grad, w_down, ((1,), (1,))).astype(jnp.bfloat16)
    down_part = dot(hidden, joint_grad, ((0,), (0,)))
    packed = with_gain(down_part.reshape(n_z, -1, width), gain_group.reshape(n_z, -1))
    arrived = lax.all_to_all(packed, "z", 0, 0, tiled=True).astype(jnp.float32)
    down_sum, gain_sum = parted(jnp.sum(arrived, axis=0), width)
    packed = with_gain(down_sum, gain_sum)
    near = packed.shape[0]
    up_rows = up_sum.shape[0] // n_yh
    up_cut = up_sum.reshape(n_yh, up_rows, -1, LANES).transpose(0, 2, 1, 3)
    up_cut = up_cut.reshape(n_yh, -1, LANES)
    up_cut = jnp.pad(up_cut, [(0, 0), (0, 0), (0, packed.shape[1] - LANES)])
    copies = jnp.broadcast_to(packed[None], (n_yh,) + packed.shape)
    both = jnp.concatenate([copies, up_cut], axis=1)
    arrived = lax.all_to_all(both, "yh", 0, 0, tiled=True)
    up_grad = jnp.sum(arrived[:, near:, :LANES].astype(jnp.float32), axis=0)
    up_grad = up_grad.reshape(-1, up_rows, LANES).transpose(1, 0, 2)
    up_grad = up_grad.reshape(up_rows, -1).astype(jnp.bfloat16)
    down_sum, gain_sum = parted(jnp.sum(arrived[:, :near].astype(jnp.float32), axis=0), width)
    arrived = spread(with_gain(down_sum, gain_sum), "z", n_z)
    down_grad, gain_grad = parted(arrived, width)
    return (hidden_grad, down_grad.reshape(-1, width), gain_grad.reshape(-1), up_grad)


def solution(mesh):
    n_z, n_yh, n_x, n_yl, n_core = (8, 4, 4, 2, 2)
    fine = Mesh(mesh.devices.reshape(n_z, n_yh, n_x, n_yl, n_core), ALL)

    def shards(*args):
        return body((n_z, n_yh, n_x * n_yl * n_core), *args)

    return jax.shard_map(
        shards,
        mesh=fine,
        in_specs=(P(DP, TENSOR), P(TENSOR, None), P(), P(DP, TENSOR), P(DP, TENSOR), P(DP, None)),
        out_specs=(P(DP, TENSOR), P(TENSOR, None), P(), P(DP, TENSOR)),
        check_vma=False,
    )
```

profile of v0, /device:TPU:23, one launch (start us, length us, event | category | flops | bytes accessed | tf_op | source)
XLA Modules:
  0.0 202.4 jit_solution(13560294213130005437)
XLA Ops:
  7.2 1.7 broadcast_in_dim.12
  8.9 6.9 %all-to-all-start.1 = ((bf16[4,16,2048]{2,1,0:T(8,128)(2,1)}), bf16[4,16,2048]{2,1,0:T(8,128)(2,1)S(1)}, u32[]{:S(2)}, u32[]{:S(2)}) async-start(bf16[4,16,2048]{2,1,0:T(8,128)(2,1)} %broadcast_in_dim.12), calls=%async_computation.1 | async-start | bytes 524288 | tf_op jit(solution)/shard_map/all_to_all | solution.py:32
  15.8 2.6 %fusion.2 = f32[512,512]{1,0:T(8,128)} fusion(bf16[512,448]{0,1:T(8,128)(2,1)} %param.6, bf16[448,576]{1,0:T(8,128)(2,1)} %param.7), kind=kOutput, calls=%fused_computation.12 | convolution fusion | flops 234881024 | bytes 1966080 | tf_op jit(solution)/shard_map/dot_general | solution.py:15
  18.4 7.4 %all-to-all-done.1 = bf16[4,16,2048]{2,1,0:T(8,128)(2,1)S(1)} async-done(((bf16[4,16,2048]{2,1,0:T(8,128)(2,1)}), bf16[4,16,2048]{2,1,0:T(8,128)(2,1)S(1)}, u32[]{:S(2)}, u32[]{:S(2)}) %all-to-all-start.1) | async-done | bytes 262176 | tf_op jit(solution)/shard_map/all_to_all | solution.py:32
  25.8 5.3 %all-to-all-start = ((f32[16,32,512]{2,1,0:T(8,128)}), f32[16,32,512]{2,1,0:T(8,128)S(1)}, u32[]{:S(2)}, u32[]{:S(2)}) async-start(f32[16,32,512]{2,1,0:T(8,128)} %bitcast.28), calls=%async_computation | async-start | bytes 2097152 | tf_op jit(solution)/shard_map/all_to_all | solution.py:26
  31.1 0.7 all-gather.2.cloned.1.call-update
  31.8 13.0 %all-to-all-done = f32[16,32,512]{2,1,0:T(8,128)S(1)} async-done(((f32[16,32,512]{2,1,0:T(8,128)}), f32[16,32,512]{2,1,0:T(8,128)S(1)}, u32[]{:S(2)}, u32[]{:S(2)}) %all-to-all-start) | async-done | bytes 1048608 | tf_op jit(solution)/shard_map/all_to_all | solution.py:26
  44.8 0.1 reduce_sum.86
  44.9 0.1 multiply_reduce_fusion.2
  45.0 0.1 multiply_convert_fusion
  45.2 13.3 %all_to_all.40 = bf16[16,32,512]{2,1,0:T(8,128)(2,1)S(1)} all-to-all(bf16[16,32,512]{2,1,0:T(8,128)(2,1)S(1)} %broadcast_in_dim.13), channel_id=1, replica_groups=mesh['z'=8,'yh'=4,'x'=4,'yl'=2,'core'=2] {'x','yl','core'}, dimensions={0} | all-to-all | bytes 1048576 | tf_op jit(solution)/shard_map/all_to_all | solution.py:32
  58.4 2.6 %convolution_convert_fusion = bf16[512,2048]{1,0:T(8,128)(2,1)} fusion(bf16[512,512]{1,0:T(8,128)(2,1)S(1)} %bitcast.35, bf16[512,2048]{1,0:T(8,128)(2,1)S(1)} %copy-done), kind=kOutput, calls=%fused_computation | convolution fusion | flops 1074790400 | bytes 4718592 | tf_op jit(solution)/shard_map/dot_general | solution.py:15
  61.1 15.9 %all-gather.2.cloned.1.call-done = bf16[512,2048]{1,0:T(8,128)(2,1)} async-done(((bf16[64,2048]{1,0:T(8,128)(2,1)}), bf16[512,2048]{1,0:T(8,128)(2,1)}) %all-gather.2.cloned.1.call-update) | async-done | bytes 2097168 | tf_op jit(solution)/shard_map/all_gather | solution.py:56
  77.0 3.7 %convolution_convert_fusion.2 = bf16[512,512]{0,1:T(8,128)(2,1)} fusion(bf16[512,2048]{1,0:T(8,128)(2,1)} %all-gather.2.cloned.1.call-done, bf16[512,2048]{1,0:T(8,128)(2,1)S(1)} %copy-done), kind=kOutput, calls=%fused_computation.2 | convolution fusion | flops 1074003968 | bytes 4718592 | tf_op jit(solution)/shard_map/dot_general | solution.py:15
  80.6 10.1 %all-to-all-start.3 = ((bf16[16,32,512]{2,1,0:T(8,128)(2,1)}), bf16[16,32,512]{2,1,0:T(8,128)(2,1)S(1)}, u32[]{:S(2)}, u32[]{:S(2)}) async-start(bf16[16,32,512]{2,1,0:T(8,128)(2,1)} %bitcast.4), calls=%async_computation.3 | async-start | bytes 1048576 | tf_op jit(solution)/shard_map/all_to_all | solution.py:26
  90.8 0.7 reduce-scatter.2.cloned.1.call-update
  91.5 0.1 pad.38.clone
  91.6 6.9 %all-to-all-done.3 = bf16[16,32,512]{2,1,0:T(8,128)(2,1)S(1)} async-done(((bf16[16,32,512]{2,1,0:T(8,128)(2,1)}), bf16[16,32,512]{2,1,0:T(8,128)(2,1)S(1)}, u32[]{:S(2)}, u32[]{:S(2)}) %all-to-all-start.3) | async-done | bytes 524320 | tf_op jit(solution)/shard_map/all_to_all | solution.py:26
  98.5 0.1 convert_reduce_fusion.1
  98.6 0.1 multiply_reduce_fusion.1
  98.8 0.1 subtract_convert_fusion
  98.9 0.1 maximum_maximum_fusion
  98.9 0.9 broadcast_in_dim.15
  99.8 6.8 %all-to-all-start.4 = ((bf16[16,40,512]{2,1,0:T(8,128)(2,1)}), bf16[16,40,512]{2,1,0:T(8,128)(2,1)S(1)}, u32[]{:S(2)}, u32[]{:S(2)}) async-start(bf16[16,40,512]{2,1,0:T(8,128)(2,1)} %broadcast_in_dim.15), calls=%async_computation.4 | async-start | bytes 1310720 | tf_op jit(solution)/shard_map/all_to_all | solution.py:32
  106.6 0.1 copy.27
  106.7 9.4 %all-to-all-done.4 = bf16[16,40,512]{2,1,0:T(8,128)(2,1)S(1)} async-done(((bf16[16,40,512]{2,1,0:T(8,128)(2,1)}), bf16[16,40,512]{2,1,0:T(8,128)(2,1)S(1)}, u32[]{:S(2)}, u32[]{:S(2)}) %all-to-all-start.4) | async-done | bytes 655392 | tf_op jit(solution)/shard_map/all_to_all | solution.py:32
  116.2 0.1 reshape.143
  116.4 0.7 copy-done.2
  117.2 0.5 convolution_convert_fusion.1
  117.7 0.9 pad_maximum_fusion.1
  118.6 3.9 %all-to-all-start.5 = ((bf16[8,56,640]{2,1,0:T(8,128)(2,1)}), bf16[8,56,640]{2,1,0:T(8,128)(2,1)S(1)}, u32[]{:S(2)}, u32[]{:S(2)}) async-start(bf16[8,56,640]{2,1,0:T(8,128)(2,1)} %pad_maximum_fusion.1), calls=%async_computation.5 | async-start | bytes 1146880 | tf_op jit(solution)/shard_map/all_to_all | solution.py:85
  122.5 18.2 %reduce-scatter.2.cloned.1.call-done = bf16[64,2048]{1,0:T(8,128)(2,1)} async-done(((bf16[512,2048]{1,0:T(8,128)(2,1)}), bf16[64,2048]{1,0:T(8,128)(2,1)}) %reduce-scatter.2.cloned.1.call-update) | async-done | bytes 262160 | tf_op jit(solution)/shard_map/reduce_scatter | solution.py:62
  140.6 1.1 reshape.144
  141.8 3.1 %all-to-all-done.5 = bf16[8,56,640]{2,1,0:T(8,128)(2,1)S(1)} async-done(((bf16[8,56,640]{2,1,0:T(8,128)(2,1)}), bf16[8,56,640]{2,1,0:T(8,128)(2,1)S(1)}, u32[]{:S(2)}, u32[]{:S(2)}) %all-to-all-start.5) | async-done | bytes 573472 | tf_op jit(solution)/shard_map/all_to_all | solution.py:85
  144.9 0.1 convert_reduce_fusion
  145.0 0.1 fusion.16
  145.1 0.1 pad_maximum_fusion.4
  145.3 17.1 %all_to_all.41 = bf16[4,120,640]{2,1,0:T(8,128)(2,1)S(1)} all-to-all(bf16[4,120,640]{2,1,0:T(8,128)(2,1)S(1)} %fusion.1), channel_id=1, replica_groups=mesh['z'=8,'yh'=4,'x'=4,'yl'=2,'core'=2] {'yh'}, dimensions={0} | all-to-all | bytes 1228800 | tf_op jit(solution)/shard_map/all_to_all | solution.py:95
  162.4 0.1 fusion.17
  162.5 0.1 pad_maximum_fusion.5
  162.6 0.9 broadcast_in_dim.17
  163.4 11.6 %all-to-all-start.7 = ((bf16[8,56,640]{2,1,0:T(8,128)(2,1)}), bf16[8,56,640]{2,1,0:T(8,128)(2,1)S(1)}, u32[]{:S(2)}, u32[]{:S(2)}) async-start(bf16[8,56,640]{2,1,0:T(8,128)(2,1)} %broadcast_in_dim.17), calls=%async_computation.8 | async-start | bytes 1146880 | tf_op jit(solution)/shard_map/all_to_all | solution.py:32
  175.0 2.5 %convolution_convert_fusion.3 = bf16[512,448]{0,1:T(8,128)(2,1)} fusion(bf16[448,576]{1,0:T(8,128)(2,1)} %param.7, bf16[512,64]{1,0:T(8,128)(2,1)S(1)} %copy.27, bf16[512,512]{1,0:T(8,128)(2,1)} %bitcast.34), kind=kOutput, calls=%fused_computation.3 | convolution fusion | flops 265650176 | bytes 1564672 | tf_op jit(solution)/shard_map/dot_general | solution.py:15
  177.6 0.6 copy.32
  178.2 15.8 %all-to-all-done.7 = bf16[8,56,640]{2,1,0:T(8,128)(2,1)S(1)} async-done(((bf16[8,56,640]{2,1,0:T(8,128)(2,1)}), bf16[8,56,640]{2,1,0:T(8,128)(2,1)S(1)}, u32[]{:S(2)}, u32[]{:S(2)}) %all-to-all-start.7) | async-done | bytes 573472 | tf_op jit(solution)/shard_map/all_to_all | solution.py:32
  194.0 0.1 slice_convert_fusion.2
  194.1 0.7 add.43
  194.8 0.8 copy.35
  (33 shorter events, 0.6 us)
Async XLA Ops:
  7.2 51.3 %copy-start = (bf16[512,2048]{1,0:T(8,128)(2,1)S(1)}, bf16[512,2048]{1,0:T(8,128)(2,1)}, u32[]{:S(2)}) copy-start(bf16[512,2048]{1,0:T(8,128)(2,1)} %param.10) | copy-start | bytes 6291460
  8.9 16.9 %all-to-all-start.1 = ((bf16[4,16,2048]{2,1,0:T(8,128)(2,1)}), bf16[4,16,2048]{2,1,0:T(8,128)(2,1)S(1)}, u32[]{:S(2)}, u32[]{:S(2)}) async-start(bf16[4,16,2048]{2,1,0:T(8,128)(2,1)} %broadcast_in_dim.12), calls=%async_computation.1 | async-start | bytes 524288 | tf_op jit(solution)/shard_map/all_to_all | solution.py:32
  25.8 5.4 %copy-start.1 = (bf16[4,16,2048]{2,1,0:T(8,128)(2,1)}, bf16[4,16,2048]{2,1,0:T(8,128)(2,1)S(1)}, u32[]{:S(2)}) copy-start(bf16[4,16,2048]{2,1,0:T(8,128)(2,1)S(1)} %all-to-all-done.1) | copy-start | bytes 786436
  25.8 19.2 %copy-start.5 = (f32[512]{0:T(512)S(1)}, f32[512]{0:T(512)}, u32[]{:S(2)}) copy-start(f32[512]{0:T(512)} %param.8) | copy-start | bytes 6148
  25.8 19.0 %all-to-all-start = ((f32[16,32,512]{2,1,0:T(8,128)}), f32[16,32,512]{2,1,0:T(8,128)S(1)}, u32[]{:S(2)}, u32[]{:S(2)}) async-start(f32[16,32,512]{2,1,0:T(8,128)} %bitcast.28), calls=%async_computation | async-start | bytes 2097152 | tf_op jit(solution)/shard_map/all_to_all | solution.py:26
  31.1 45.9 %all-gather.2.cloned.1.call-start = ((), (), s32[]{:S(2)}) async-start(), calls=%async_computation.9 | async-start | bytes 2359296 | tf_op jit(solution)/shard_map/all_gather | solution.py:56
  80.6 17.9 %all-to-all-start.3 = ((bf16[16,32,512]{2,1,0:T(8,128)(2,1)}), bf16[16,32,512]{2,1,0:T(8,128)(2,1)S(1)}, u32[]{:S(2)}, u32[]{:S(2)}) async-start(bf16[16,32,512]{2,1,0:T(8,128)(2,1)} %bitcast.4), calls=%async_computation.3 | async-start | bytes 1048576 | tf_op jit(solution)/shard_map/all_to_all | solution.py:26
  90.8 49.9 %reduce-scatter.2.cloned.1.call-start = ((), (), s32[]{:S(2)}) async-start(), calls=%async_computation.10 | async-start | bytes 2359296 | tf_op jit(solution)/shard_map/reduce_scatter | solution.py:62
  98.6 8.0 %copy-start.4 = (bf16[512,64]{0,1:T(8,128)(2,1)S(1)}, bf16[512,64]{0,1:T(8,128)(2,1)}, u32[]{:S(2)}) copy-start(bf16[512,64]{0,1:T(8,128)(2,1)} %param.11) | copy-start | bytes 196612
  99.8 17.3 %copy-start.3 = (bf16[512,448]{0,1:T(8,128)(2,1)S(1)}, bf16[512,448]{0,1:T(8,128)(2,1)}, u32[]{:S(2)}) copy-start(bf16[512,448]{0,1:T(8,128)(2,1)} %param.6) | copy-start | bytes 1376260
  99.8 16.3 %all-to-all-start.4 = ((bf16[16,40,512]{2,1,0:T(8,128)(2,1)}), bf16[16,40,512]{2,1,0:T(8,128)(2,1)S(1)}, u32[]{:S(2)}, u32[]{:S(2)}) async-start(bf16[16,40,512]{2,1,0:T(8,128)(2,1)} %broadcast_in_dim.15), calls=%async_computation.4 | async-start | bytes 1310720 | tf_op jit(solution)/shard_map/all_to_all | solution.py:32
  116.3 0.8 copy-start.2
  118.6 26.3 %all-to-all-start.5 = ((bf16[8,56,640]{2,1,0:T(8,128)(2,1)}), bf16[8,56,640]{2,1,0:T(8,128)(2,1)S(1)}, u32[]{:S(2)}, u32[]{:S(2)}) async-start(bf16[8,56,640]{2,1,0:T(8,128)(2,1)} %pad_maximum_fusion.1), calls=%async_computation.5 | async-start | bytes 1146880 | tf_op jit(solution)/shard_map/all_to_all | solution.py:85
  163.4 30.6 %all-to-all-start.7 = ((bf16[8,56,640]{2,1,0:T(8,128)(2,1)}), bf16[8,56,640]{2,1,0:T(8,128)(2,1)S(1)}, u32[]{:S(2)}, u32[]{:S(2)}) async-start(bf16[8,56,640]{2,1,0:T(8,128)(2,1)} %broadcast_in_dim.17), calls=%async_computation.8 | async-start | bytes 1146880 | tf_op jit(solution)/shard_map/all_to_all | solution.py:32
Sparse Core Ops, SparseCore 0:
  34.6 42.3 all-gather.1
  94.4 46.1 reduce-scatter.1
where the time goes:
time: 203 us; the launch traced here: 202 us
  waiting for transfers between devices  91.1 us (45%)
  starting transfers between devices  44.6 us (22%)
  blocking collectives  30.4 us (15%)
  between operations  14.2 us (7%)
  matrix products  12 us (6%)
  local copies, waits for them, and re-layouts  7.94 us (4%)
  other arithmetic  2.25 us (1%)
    all_to_all x3, waiting for transfers between devices, spread(): return lax.all_to_all(copies, axes, 0, 0, tiled=True)  32.6 us
    all_to_all x3, starting transfers between devices, spread(): return lax.all_to_all(copies, axes, 0, 0, tiled=True)  25.3 us
    all_to_all x2, waiting for transfers between devices, scatter_sum(): arrived = lax.all_to_all(pieces, axes, 0, 0, tiled=True)  19.9 us
    reduce_scatter x1, waiting for transfers between devices, body(): up_sum = lax.psum_scatter(up_part, 'z', scatter_dimension=0, tiled=True)  18.2 us
    all_to_all x1, blocking collectives, body(): arrived = lax.all_to_all(both, 'yh', 0, 0, tiled=True)  17.1 us
    all_gather x1, waiting for transfers between devices, body(): w_up_all = lax.all_gather(w_up_near, 'z', axis=0, tiled=True)  15.9 us
    all_to_all x2, starting transfers between devices, scatter_sum(): arrived = lax.all_to_all(pieces, axes, 0, 0, tiled=True)  15.4 us
    all_to_all x1, blocking collectives, spread(): return lax.all_to_all(copies, axes, 0, 0, tiled=True)  13.3 us
  transfers between devices with their start and end apart: 8, of which 8 were waited for; matrix products, arithmetic and copies ran while one was open for 6% of the time, Pallas kernels for 0%

commit v1 on v0

--- a/solution.py
+++ b/solution.py
@@ -53,7 +53,9 @@
     lat = norm_gain.shape[0]
     width = w_down.shape[1]
     w_up_near = spread(w_up, "yh", n_yh).reshape(-1, w_up.shape[1])
-    w_up_all = lax.all_gather(w_up_near, "z", axis=0, tiled=True)
+    w_up_all = jnp.concatenate(
+        lax.all_to_all(jnp.stack([w_up_near] * lax.axis_size("z")), "z", 0, 0), axis=0
+    )
     projected = scatter_sum(dot(hidden, w_down[:, :lat], ((1,), (0,))), TENSOR, n_t)
     inv_rms = lax.rsqrt(jnp.mean(projected * projected, axis=1, keepdims=True) + 1e-06)
     latent = (projected * inv_rms * norm_gain).astype(jnp.bfloat16)

time: 203 us -> 240 us (1.18)
  the two profiles are of different devices: /device:TPU:23 before, /device:TPU:17 now
where the time goes in v1:
time: 240 us; the launch traced here: 239 us
  waiting for transfers between devices  108 us (45%)
  blocking collectives  63.3 us (26%)
  starting transfers between devices  32.1 us (13%)
  between operations  14.2 us (6%)
  matrix products  11.1 us (5%)
  local copies, waits for them, and re-layouts  8.53 us (4%)
    all_to_all x1, waiting for transfers between devices, body(): lax.all_to_all(jnp.stack([w_up_near] * lax.axis_size('z')), 'z', 0, 0)  48.8 us
    all_to_all x3, waiting for transfers between devices, spread(): return lax.all_to_all(copies, axes, 0, 0, tiled=True)  32.6 us
    all_to_all x1, blocking collectives, body(): arrived = lax.all_to_all(both, 'yh', 0, 0, tiled=True)  25 us
    all_to_all x1, blocking collectives, scatter_sum(): arrived = lax.all_to_all(pieces, axes, 0, 0, tiled=True)  21.3 us
    all_to_all x1, blocking collectives, spread(): return lax.all_to_all(copies, axes, 0, 0, tiled=True)  16.9 us
    all_to_all x3, starting transfers between devices, spread(): return lax.all_to_all(copies, axes, 0, 0, tiled=True)  14.4 us
    dot_general x5, matrix products, dot(): lax.dot_general(a, b, (dims, ((), ())), preferred_element_type=jnp.float32)  11.1 us
    all_to_all x1, waiting for transfers between devices, body(): arrived = lax.all_to_all(packed, 'z', 0, 0, tiled=True).astype(jnp.float32)  10.1 us
  transfers between devices with their start and end apart: 7, of which 7 were waited for; matrix products, arithmetic and copies ran while one was open for 4% of the time, Pallas kernels for 0%

profile of v1, /device:TPU:17, one launch (start us, length us, event | category | flops | bytes accessed | tf_op | source)
XLA Modules:
  0.0 239.2 jit_solution(6658999956530890991)
XLA Ops:
  7.2 1.8 fusion.2
  9.0 21.3 %all_to_all.45 = f32[16,32,512]{2,1,0:T(8,128)S(1)} all-to-all(f32[16,32,512]{2,1,0:T(8,128)S(1)} %bitcast.29), channel_id=1, replica_groups=mesh['z'=8,'yh'=4,'x'=4,'yl'=2,'core'=2] {'x','yl','core'}, dimensions={0} | all-to-all | bytes 2097152 | tf_op jit(solution)/shard_map/all_to_all | solution.py:26
  30.3 0.7 broadcast_in_dim.12
  31.0 6.2 %all-to-all-start.1 = ((bf16[4,16,2048]{2,1,0:T(8,128)(2,1)}), bf16[4,16,2048]{2,1,0:T(8,128)(2,1)S(1)}, u32[]{:S(2)}, u32[]{:S(2)}) async-start(bf16[4,16,2048]{2,1,0:T(8,128)(2,1)} %broadcast_in_dim.12), calls=%async_computation.1 | async-start | bytes 524288 | tf_op jit(solution)/shard_map/all_to_all | solution.py:32
  37.2 0.1 reduce_sum.86
  37.3 0.1 multiply_reduce_fusion.2
  37.4 0.1 multiply_convert_fusion
  37.5 5.7 %all-to-all-done.1 = bf16[4,16,2048]{2,1,0:T(8,128)(2,1)S(1)} async-done(((bf16[4,16,2048]{2,1,0:T(8,128)(2,1)}), bf16[4,16,2048]{2,1,0:T(8,128)(2,1)S(1)}, u32[]{:S(2)}, u32[]{:S(2)}) %all-to-all-start.1) | async-done | bytes 262176 | tf_op jit(solution)/shard_map/all_to_all | solution.py:32
  43.3 16.9 %all_to_all.46 = bf16[16,32,512]{2,1,0:T(8,128)(2,1)S(1)} all-to-all(bf16[16,32,512]{2,1,0:T(8,128)(2,1)S(1)} %broadcast_in_dim.13), channel_id=1, replica_groups=mesh['z'=8,'yh'=4,'x'=4,'yl'=2,'core'=2] {'x','yl','core'}, dimensions={0} | all-to-all | bytes 1048576 | tf_op jit(solution)/shard_map/all_to_all | solution.py:32
  60.3 1.6 stack.8
  61.8 9.8 %all-to-all-start.2 = ((bf16[8,64,2048]{2,1,0:T(8,128)(2,1)}), bf16[8,64,2048]{2,1,0:T(8,128)(2,1)}, u32[]{:S(2)}, u32[]{:S(2)}) async-start(bf16[8,64,2048]{2,1,0:T(8,128)(2,1)} %stack.8), calls=%async_computation.2 | async-start | bytes 4194304 | tf_op jit(solution)/shard_map/all_to_all | solution.py:57
  71.6 2.6 %convolution_convert_fusion = bf16[512,2048]{1,0:T(8,128)(2,1)} fusion(bf16[512,512]{1,0:T(8,128)(2,1)S(1)} %bitcast.36, bf16[512,2048]{1,0:T(8,128)(2,1)S(1)} %copy-done), kind=kOutput, calls=%fused_computation | convolution fusion | flops 1074790400 | bytes 4718592 | tf_op jit(solution)/shard_map/dot_general | solution.py:15
  74.3 48.8 %all-to-all-done.2 = bf16[8,64,2048]{2,1,0:T(8,128)(2,1)} async-done(((bf16[8,64,2048]{2,1,0:T(8,128)(2,1)}), bf16[8,64,2048]{2,1,0:T(8,128)(2,1)}, u32[]{:S(2)}, u32[]{:S(2)}) %all-to-all-start.2) | async-done | bytes 2097184 | tf_op jit(solution)/shard_map/all_to_all | solution.py:57
  123.0 3.7 %convolution_convert_fusion.2 = bf16[512,512]{0,1:T(8,128)(2,1)} fusion(bf16[512,2048]{1,0:T(8,128)(2,1)} %bitcast.2, bf16[512,2048]{1,0:T(8,128)(2,1)S(1)} %copy-done), kind=kOutput, calls=%fused_computation.2 | convolution fusion | flops 1074003968 | bytes 4718592 | tf_op jit(solution)/shard_map/dot_general | solution.py:15
  126.7 4.3 %all-to-all-start.4 = ((bf16[16,32,512]{2,1,0:T(8,128)(2,1)}), bf16[16,32,512]{2,1,0:T(8,128)(2,1)S(1)}, u32[]{:S(2)}, u32[]{:S(2)}) async-start(bf16[16,32,512]{2,1,0:T(8,128)(2,1)} %bitcast.5), calls=%async_computation.4 | async-start | bytes 1048576 | tf_op jit(solution)/shard_map/all_to_all | solution.py:26
  131.1 0.7 reduce-scatter.2.cloned.1.call-update
  131.8 0.1 pad.38.clone
  131.8 9.1 %all-to-all-done.4 = bf16[16,32,512]{2,1,0:T(8,128)(2,1)S(1)} async-done(((bf16[16,32,512]{2,1,0:T(8,128)(2,1)}), bf16[16,32,512]{2,1,0:T(8,128)(2,1)S(1)}, u32[]{:S(2)}, u32[]{:S(2)}) %all-to-all-start.4) | async-done | bytes 524320 | tf_op jit(solution)/shard_map/all_to_all | solution.py:26
  140.9 0.1 convert_reduce_fusion.1
  141.0 0.1 multiply_reduce_fusion.1
  141.1 0.1 subtract_convert_fusion
  141.2 0.1 maximum_maximum_fusion
  141.3 0.9 broadcast_in_dim.15
  142.2 4.7 %all-to-all-start.5 = ((bf16[16,40,512]{2,1,0:T(8,128)(2,1)}), bf16[16,40,512]{2,1,0:T(8,128)(2,1)S(1)}, u32[]{:S(2)}, u32[]{:S(2)}) async-start(bf16[16,40,512]{2,1,0:T(8,128)(2,1)} %broadcast_in_dim.15), calls=%async_computation.5 | async-start | bytes 1310720 | tf_op jit(solution)/shard_map/all_to_all | solution.py:32
  146.9 0.1 copy.27
  147.0 11.2 %all-to-all-done.5 = bf16[16,40,512]{2,1,0:T(8,128)(2,1)S(1)} async-done(((bf16[16,40,512]{2,1,0:T(8,128)(2,1)}), bf16[16,40,512]{2,1,0:T(8,128)(2,1)S(1)}, u32[]{:S(2)}, u32[]{:S(2)}) %all-to-all-start.5) | async-done | bytes 655392 | tf_op jit(solution)/shard_map/all_to_all | solution.py:32
  158.3 0.1 reshape.145
  158.5 0.7 copy-done.1
  159.2 0.5 convolution_convert_fusion.1
  159.7 0.9 pad_maximum_fusion.1
  160.6 3.5 %all-to-all-start.6 = ((bf16[8,56,640]{2,1,0:T(8,128)(2,1)}), bf16[8,56,640]{2,1,0:T(8,128)(2,1)S(1)}, u32[]{:S(2)}, u32[]{:S(2)}) async-start(bf16[8,56,640]{2,1,0:T(8,128)(2,1)} %pad_maximum_fusion.1), calls=%async_computation.6 | async-start | bytes 1146880 | tf_op jit(solution)/shard_map/all_to_all | solution.py:87
  164.2 6.3 %reduce-scatter.2.cloned.1.call-done = bf16[64,2048]{1,0:T(8,128)(2,1)} async-done(((bf16[512,2048]{1,0:T(8,128)(2,1)}), bf16[64,2048]{1,0:T(8,128)(2,1)}) %reduce-scatter.2.cloned.1.call-update) | async-done | bytes 262160 | tf_op jit(solution)/shard_map/reduce_scatter | solution.py:64
  170.5 1.1 reshape.146
  171.7 10.1 %all-to-all-done.6 = bf16[8,56,640]{2,1,0:T(8,128)(2,1)S(1)} async-done(((bf16[8,56,640]{2,1,0:T(8,128)(2,1)}), bf16[8,56,640]{2,1,0:T(8,128)(2,1)S(1)}, u32[]{:S(2)}, u32[]{:S(2)}) %all-to-all-start.6) | async-done | bytes 573472 | tf_op jit(solution)/shard_map/all_to_all | solution.py:87
  181.8 0.1 convert_reduce_fusion
  181.9 0.1 fusion.16
  182.0 0.1 pad_maximum_fusion.4
  182.2 25.0 %all_to_all.47 = bf16[4,120,640]{2,1,0:T(8,128)(2,1)S(1)} all-to-all(bf16[4,120,640]{2,1,0:T(8,128)(2,1)S(1)} %fusion.1), channel_id=1, replica_groups=mesh['z'=8,'yh'=4,'x'=4,'yl'=2,'core'=2] {'yh'}, dimensions={0} | all-to-all | bytes 1228800 | tf_op jit(solution)/shard_map/all_to_all | solution.py:97
  207.2 0.1 fusion.17
  207.3 0.1 pad_maximum_fusion.5
  207.4 0.9 broadcast_in_dim.17
  208.3 3.5 %all-to-all-start.8 = ((bf16[8,56,640]{2,1,0:T(8,128)(2,1)}), bf16[8,56,640]{2,1,0:T(8,128)(2,1)S(1)}, u32[]{:S(2)}, u32[]{:S(2)}) async-start(bf16[8,56,640]{2,1,0:T(8,128)(2,1)} %broadcast_in_dim.17), calls=%async_computation.9 | async-start | bytes 1146880 | tf_op jit(solution)/shard_map/all_to_all | solution.py:32
  211.8 2.5 %convolution_convert_fusion.3 = bf16[512,448]{0,1:T(8,128)(2,1)} fusion(bf16[448,576]{1,0:T(8,128)(2,1)} %param.7, bf16[512,64]{1,0:T(8,128)(2,1)S(1)} %copy.27, bf16[512,512]{1,0:T(8,128)(2,1)} %bitcast.35), kind=kOutput, calls=%fused_computation.3 | convolution fusion | flops 265650176 | bytes 1564672 | tf_op jit(solution)/shard_map/dot_general | solution.py:15
  214.4 0.6 copy.32
  215.0 15.7 %all-to-all-done.8 = bf16[8,56,640]{2,1,0:T(8,128)(2,1)S(1)} async-done(((bf16[8,56,640]{2,1,0:T(8,128)(2,1)}), bf16[8,56,640]{2,1,0:T(8,128)(2,1)S(1)}, u32[]{:S(2)}, u32[]{:S(2)}) %all-to-all-start.8) | async-done | bytes 573472 | tf_op jit(solution)/shard_map/all_to_all | solution.py:32
  230.7 0.1 slice_convert_fusion.2
  230.8 0.7 add.43
  231.5 0.8 copy.35
  (32 shorter events, 0.5 us)
Async XLA Ops:
  7.2 64.5 %copy-start = (bf16[512,2048]{1,0:T(8,128)(2,1)S(1)}, bf16[512,2048]{1,0:T(8,128)(2,1)}, u32[]{:S(2)}) copy-start(bf16[512,2048]{1,0:T(8,128)(2,1)} %param.10) | copy-start | bytes 6291460
  9.0 21.4 %copy-start.3 = (bf16[16,2048]{1,0:T(8,128)(2,1)S(1)}, bf16[16,2048]{1,0:T(8,128)(2,1)}, u32[]{:S(2)}) copy-start(bf16[16,2048]{1,0:T(8,128)(2,1)} %param.9) | copy-start | bytes 196612
  30.3 7.1 %copy-start.5 = (f32[512]{0:T(512)S(1)}, f32[512]{0:T(512)}, u32[]{:S(2)}) copy-start(f32[512]{0:T(512)} %param.8) | copy-start | bytes 6148
  31.0 12.2 %all-to-all-start.1 = ((bf16[4,16,2048]{2,1,0:T(8,128)(2,1)}), bf16[4,16,2048]{2,1,0:T(8,128)(2,1)S(1)}, u32[]{:S(2)}, u32[]{:S(2)}) async-start(bf16[4,16,2048]{2,1,0:T(8,128)(2,1)} %broadcast_in_dim.12), calls=%async_computation.1 | async-start | bytes 524288 | tf_op jit(solution)/shard_map/all_to_all | solution.py:32
  61.8 61.2 %all-to-all-start.2 = ((bf16[8,64,2048]{2,1,0:T(8,128)(2,1)}), bf16[8,64,2048]{2,1,0:T(8,128)(2,1)}, u32[]{:S(2)}, u32[]{:S(2)}) async-start(bf16[8,64,2048]{2,1,0:T(8,128)(2,1)} %stack.8), calls=%async_computation.2 | async-start | bytes 4194304 | tf_op jit(solution)/shard_map/all_to_all | solution.py:57
  126.7 14.2 %all-to-all-start.4 = ((bf16[16,32,512]{2,1,0:T(8,128)(2,1)}), bf16[16,32,512]{2,1,0:T(8,128)(2,1)S(1)}, u32[]{:S(2)}, u32[]{:S(2)}) async-start(bf16[16,32,512]{2,1,0:T(8,128)(2,1)} %bitcast.5), calls=%async_computation.4 | async-start | bytes 1048576 | tf_op jit(solution)/shard_map/all_to_all | solution.py:26
  131.0 39.5 %reduce-scatter.2.cloned.1.call-start = ((), (), s32[]{:S(2)}) async-start(), calls=%async_computation.10 | async-start | bytes 2359296 | tf_op jit(solution)/shard_map/reduce_scatter | solution.py:64
  141.0 5.9 %copy-start.4 = (bf16[512,64]{0,1:T(8,128)(2,1)S(1)}, bf16[512,64]{0,1:T(8,128)(2,1)}, u32[]{:S(2)}) copy-start(bf16[512,64]{0,1:T(8,128)(2,1)} %param.11) | copy-start | bytes 196612
  142.2 17.0 %copy-start.2 = (bf16[512,448]{0,1:T(8,128)(2,1)S(1)}, bf16[512,448]{0,1:T(8,128)(2,1)}, u32[]{:S(2)}) copy-start(bf16[512,448]{0,1:T(8,128)(2,1)} %param.6) | copy-start | bytes 1376260
  142.2 16.0 %all-to-all-start.5 = ((bf16[16,40,512]{2,1,0:T(8,128)(2,1)}), bf16[16,40,512]{2,1,0:T(8,128)(2,1)S(1)}, u32[]{:S(2)}, u32[]{:S(2)}) async-start(bf16[16,40,512]{2,1,0:T(8,128)(2,1)} %broadcast_in_dim.15), calls=%async_computation.5 | async-start | bytes 1310720 | tf_op jit(solution)/shard_map/all_to_all | solution.py:32
  158.4 0.8 copy-start.1
  160.6 21.1 %all-to-all-start.6 = ((bf16[8,56,640]{2,1,0:T(8,128)(2,1)}), bf16[8,56,640]{2,1,0:T(8,128)(2,1)S(1)}, u32[]{:S(2)}, u32[]{:S(2)}) async-start(bf16[8,56,640]{2,1,0:T(8,128)(2,1)} %pad_maximum_fusion.1), calls=%async_computation.6 | async-start | bytes 1146880 | tf_op jit(solution)/shard_map/all_to_all | solution.py:87
  208.3 22.5 %all-to-all-start.8 = ((bf16[8,56,640]{2,1,0:T(8,128)(2,1)}), bf16[8,56,640]{2,1,0:T(8,128)(2,1)S(1)}, u32[]{:S(2)}, u32[]{:S(2)}) async-start(bf16[8,56,640]{2,1,0:T(8,128)(2,1)} %broadcast_in_dim.17), calls=%async_computation.9 | async-start | bytes 1146880 | tf_op jit(solution)/shard_map/all_to_all | solution.py:32
Sparse Core Ops, SparseCore 0:
  134.7 35.7 reduce-scatter.1
